TPU v7x, 128 devices: a whole 4x4x4 slice. The times are simulated.
128 devices in a mesh: frame: 16 (over y, x), head: 8 (over z, core).
Axes of the slice: x: 4, y: 4, z: 4, core: 2. Of those that a mesh axis runs over, the one named last changes fastest.
Arguments:
- tokens: bfloat16 [12288, 5120], P('frame', 'head'), may hold values from -40 to 40
- mask_block_frame: int32 [96], replicated, may hold values from 0 to 7, as said below
- attended_key_blocks: int32 [96, 10], replicated, may hold values from 0 to 95, as said below
- frozen_query_key_value: bfloat16 [5120, 3, 3072], P(None, None, 'head'), may hold values from -0.104815686 to 0.104815686
- query_key_value_down_weight: bfloat16 [5120, 192], replicated, may hold values from -0.078125 to 0.078125
- query_key_value_up_weight: bfloat16 [64, 3, 3072], P(None, None, 'head'), may hold values from -0.375 to 0.375
- frozen_output_weight: bfloat16 [3072, 5120], P('head'), may hold values from -0.109375 to 0.109375
- output_down_weight: bfloat16 [3072, 64], P('head'), may hold values from -0.109375 to 0.109375
- output_up_weight: bfloat16 [64, 5120], P(None, 'head'), may hold values from -0.75 to 0.75
Outputs:
- attended_out: bfloat16 [12288, 5120], P('frame', 'head')
Inputs may be any that keep to these rules, and one draw needn't show every extreme that they name: `mask_block_frame`: Non-decreasing along the blocks; every frame from 0 to 7 holds at least one block. `attended_key_blocks`: row b lists 10 distinct key blocks and always includes b itself. Take aligned groups of 6 blocks; for a group of query blocks and another group g groups away (g >= 1), the rows of the first group together name exactly 4 // 2 ** (g - 1) distinct blocks of the second, except that a group exactly 8 groups away is named by exactly the larger of that number and 2.
All inputs are finite; a program needn't handle non-finite values.
Results may differ from a plain program's by a relative error of at most 0.017.
Values may be sent and summed in bfloat16 or wider, within the bound.
A program may use at most 128 MiB of HBM per device.

v0:
```python
import math

import jax
import jax.numpy as jnp
from jax import lax
from jax.sharding import PartitionSpec as P

MODEL_WIDTH = 5120
HEAD_SIZE = 128
BLOCK = 128


def rotate_pairs(values, frame_pos, place):
    time_pairs = (HEAD_SIZE - 4 * (HEAD_SIZE // 6)) // 2
    space_pairs = (HEAD_SIZE - 2 * time_pairs) // 2
    time_freq = 10000.0 ** (-jnp.arange(time_pairs).astype(jnp.float32) / time_pairs)
    space_freq = 10000.0 ** (-jnp.arange(space_pairs).astype(jnp.float32) / space_pairs)
    time_angle = frame_pos[:, None] * time_freq[None, :]
    space_angle = place[:, None] * space_freq[None, :]
    cos_time = jnp.cos(time_angle)[:, None, :]
    sin_time = jnp.sin(time_angle)[:, None, :]
    cos_space = jnp.cos(space_angle)[:, None, :]
    sin_space = jnp.sin(space_angle)[:, None, :]
    first_part = values[:, :, :time_pairs]
    second_part = values[:, :, time_pairs : 2 * time_pairs]
    third_part = values[:, :, 2 * time_pairs : 2 * time_pairs + space_pairs]
    fourth_part = values[:, :, 2 * time_pairs + space_pairs :]
    return jnp.concatenate(
        [
            first_part * cos_time - second_part * sin_time,
            first_part * sin_time + second_part * cos_time,
            third_part * cos_space - fourth_part * sin_space,
            third_part * sin_space + fourth_part * cos_space,
        ],
        axis=-1,
    )


def token_positions(mask_block_frame, block_ids):
    count_blocks = mask_block_frame.shape[0]
    all_blocks = jnp.arange(count_blocks)
    same_frame = mask_block_frame[:, None] == mask_block_frame[None, :]
    first_block = jnp.min(jnp.where(same_frame, all_blocks[None, :], count_blocks), axis=1)
    inner_ids = jnp.arange(BLOCK)
    token_ids = block_ids[:, None] * BLOCK + inner_ids[None, :]
    frame_pos = (
        jnp.broadcast_to(mask_block_frame[block_ids][:, None], token_ids.shape)
        .reshape(-1)
        .astype(jnp.float32)
    )
    place = (token_ids - first_block[block_ids][:, None] * BLOCK).reshape(-1).astype(jnp.float32)
    return (frame_pos, place)


def body(
    tokens,
    mask_block_frame,
    attended_key_blocks,
    frozen_query_key_value,
    query_key_value_down_weight,
    query_key_value_up_weight,
    frozen_output_weight,
    output_down_weight,
    output_up_weight,
):
    tok_rows = tokens.shape[0]
    blocks_here = tok_rows // BLOCK
    local_width = frozen_output_weight.shape[0]
    heads_here = local_width // HEAD_SIZE
    adapter_rank_width = output_up_weight.shape[0]
    listed = attended_key_blocks.shape[1]
    weights_flat = frozen_query_key_value.reshape(MODEL_WIDTH, 3 * local_width)
    rank_segment = lax.all_gather(tokens, "head", axis=1, tiled=True)
    projected_rows = jnp.dot(rank_segment, weights_flat, preferred_element_type=jnp.float32)
    adapter_output_sum = jnp.dot(
        rank_segment, query_key_value_down_weight, preferred_element_type=jnp.float32
    )
    adapter_query_key_value = adapter_output_sum.astype(jnp.bfloat16).reshape(
        tok_rows, 3, adapter_rank_width
    )
    projected_rows = projected_rows.reshape(tok_rows, 3, local_width) + jnp.einsum(
        "ngc,cgz->ngz",
        adapter_query_key_value,
        query_key_value_up_weight,
        preferred_element_type=jnp.float32,
    )
    frame_index = lax.axis_index("frame")
    block_ids = frame_index * blocks_here + jnp.arange(blocks_here, dtype=jnp.int32)
    frame_pos, place = token_positions(mask_block_frame, block_ids)
    queries = rotate_pairs(
        projected_rows[:, 0].reshape(tok_rows, heads_here, HEAD_SIZE), frame_pos, place
    ).astype(jnp.bfloat16)
    keys = rotate_pairs(
        projected_rows[:, 1].reshape(tok_rows, heads_here, HEAD_SIZE), frame_pos, place
    ).astype(jnp.bfloat16)
    key_tiles = keys.reshape(blocks_here, BLOCK, local_width)
    value_tiles = projected_rows[:, 2].astype(jnp.bfloat16).reshape(blocks_here, BLOCK, local_width)
    my_lists = lax.dynamic_slice_in_dim(
        attended_key_blocks, frame_index * blocks_here, blocks_here, 0
    )
    pool_keys, pool_values = (
        lax.all_gather(key_tiles, "frame", axis=0, tiled=True),
        lax.all_gather(value_tiles, "frame", axis=0, tiled=True),
    )
    chosen_keys = pool_keys[my_lists].reshape(blocks_here, listed * BLOCK, heads_here, HEAD_SIZE)
    chosen_values = pool_values[my_lists].reshape(
        blocks_here, listed * BLOCK, heads_here, HEAD_SIZE
    )
    query_tiles = queries.reshape(blocks_here, BLOCK, heads_here, HEAD_SIZE)
    scores = jnp.einsum(
        "nqhd,nkhd->nhqk", query_tiles, chosen_keys, preferred_element_type=jnp.float32
    ) / math.sqrt(HEAD_SIZE)
    row_max = jnp.max(scores, axis=-1, keepdims=True)
    powers = jnp.exp(scores - row_max)
    probs = (powers / jnp.sum(powers, axis=-1, keepdims=True)).astype(jnp.bfloat16)
    attention_result = jnp.einsum(
        "nhqk,nkhd->nqhd", probs, chosen_values, preferred_element_type=jnp.float32
    ).astype(jnp.bfloat16)
    attention_result = attention_result.reshape(tok_rows, local_width)
    adapter_output = lax.psum(
        jnp.dot(attention_result, output_down_weight, preferred_element_type=jnp.float32).astype(
            jnp.bfloat16
        ),
        "head",
    )
    partial_value = jnp.dot(
        attention_result, frozen_output_weight, preferred_element_type=jnp.float32
    )
    frozen_output = lax.psum_scatter(
        partial_value.astype(jnp.bfloat16), "head", scatter_dimension=1, tiled=True
    ).astype(jnp.float32)
    return (
        frozen_output
        + jnp.dot(adapter_output, output_up_weight, preferred_element_type=jnp.float32)
    ).astype(jnp.bfloat16)


def solution(mesh):
    return jax.shard_map(
        body,
        mesh=mesh,
        in_specs=(
            P("frame", "head"),
            P(),
            P(),
            P(None, None, "head"),
            P(),
            P(None, None, "head"),
            P("head", None),
            P("head", None),
            P(None, "head"),
        ),
        out_specs=P("frame", "head"),
        check_vma=False,
    )
```

profile of v0, /device:TPU:14, one launch (start us, length us, event | category | flops | bytes accessed | tf_op | source)
XLA Modules:
  0.0 407.1 jit_solution(18228735309528296065)
XLA Ops:
  7.3 1.3 gather_fusion.1
  10.2 16.2 %copy.37 = bf16[5120,3,384]{0,2,1:T(8,128)(2,1)} copy(bf16[5120,3,384]{2,0,1:T(8,128)(2,1)} %param.12) | data formatting | bytes 23592960 | tf_op args[3]
  27.5 31.4 %all-gather.4.cloned.1.call-done = bf16[768,5120]{1,0:T(8,128)(2,1)} async-done(((bf16[768,640]{1,0:T(8,128)(2,1)}), bf16[768,5120]{1,0:T(8,128)(2,1)}) %all-gather.4.cloned.1.call-update) | async-done | bytes 7864336 | tf_op jit(solution)/shard_map/all_gather | solution.py:73
  58.9 6.1 %convolution_convert_fusion.1 = bf16[768,192]{0,1:T(8,128)(2,1)S(1)} fusion(bf16[768,5120]{1,0:T(8,128)(2,1)} %all-gather.4.cloned.1.call-done, bf16[5120,192]{0,1:T(8,128)(2,1)S(1)} %copy-done), kind=kOutput, calls=%fused_computation.22 | convolution fusion | flops 1510096896 | bytes 10125312 | tf_op jit(solution)/shard_map/dot_general | solution.py:75
  65.7 13.3 %bitcast_add_fusion = f32[768,3,384]{0,2,1:T(8,128)S(1)} fusion(f32[3,768,384]{1,2,0:T(8,128)S(1)} %fusion.38, bf16[5120,3,384]{0,2,1:T(8,128)(2,1)S(1)} %copy-done.2, bf16[768,5120]{1,0:T(8,128)(2,1)} %all-gather.4.cloned.1.call-done), kind=kOutput, calls=%fused_computation.18 | convolution fusion | flops 9060581376 | bytes 26738688 | tf_op jit(solution)/shard_map/dot_general | solution.py:74
  79.7 1.1 copy-done.3
  81.6 1.3 copy.45
  82.9 1.3 slice.81
  84.3 1.1 copy.38
  88.2 69.0 %all-gather.8.cloned.1.call-done = bf16[96,128,384]{2,1,0:T(8,128)(2,1)} async-done(((bf16[6,128,384]{2,1,0:T(8,128)(2,1)}), bf16[96,128,384]{2,1,0:T(8,128)(2,1)}) %all-gather.8.cloned.1.call-update) | async-done | bytes 9437200 | tf_op jit(solution)/shard_map/all_gather | solution.py:102
  157.2 7.7 %gather_fusion.3 = bf16[60,128,384]{2,1,0:T(8,128)(2,1)} fusion(bf16[96,128,384]{2,1,0:T(8,128)(2,1)} %all-gather.8.cloned.1.call-done, s32[1024]{0:T(1024)S(1)} %pad_clamp_fusion.1), kind=kCustom, calls=%fused_computation.3 | custom fusion | bytes 11796720 | tf_op jit(solution)/shard_map/gather | solution.py:105
  165.0 15.9 %reshape.243 = bf16[6,1280,3,128]{3,2,1,0:T(4,128)(2,1)} reshape(bf16[60,128,384]{2,1,0:T(8,128)(2,1)} %gather_fusion.3) | data formatting | bytes 11796480 | tf_op jit(solution)/shard_map/reshape | solution.py:105
  180.9 9.3 %fusion.7 = f32[6,3,128,1280]{3,2,1,0:T(8,128)} fusion(bf16[6,1280,3,128]{3,2,1,0:T(4,128)(2,1)} %reshape.243, bf16[6,128,3,42]{3,1,2,0:T(8,128)(2,1)S(1)} %copy.44, bf16[6,128,3,42]{3,1,2,0:T(8,128)(2,1)S(1)} %copy.43, bf16[6,128,3,22]{3,1,2,0:T(8,128)(2,1)S(1)} %copy.42, bf16[6,128,3,22]{3,1,2,0:T(8,128)(2,1)S(1)} %copy.41), kind=kOutput, calls=%fused_computation.13 | convolution fusion | flops 757334016 | bytes 18284544 | tf_op jit(solution)/shard_map/nqhd,nkhd->nhqk/dot_general | solution.py:110
  190.2 15.6 %fusion.37 = (f32[6,3,128]{2,1,0:T(4,128)S(1)}, f32[6,3,128,1280]{3,2,1,0:T(8,128)}) fusion(f32[6,3,128,1280]{3,2,1,0:T(8,128)} %fusion.7), kind=kOutput, calls=%fused_computation.64 | output fusion | flops 11797759 | bytes 23602176 | tf_op jit(solution)/shard_map/sub | solution.py:114
  205.8 28.7 %all-gather.6.cloned.1.call-done = bf16[96,128,384]{2,1,0:T(8,128)(2,1)} async-done(((bf16[6,128,384]{2,1,0:T(8,128)(2,1)}), bf16[96,128,384]{2,1,0:T(8,128)(2,1)}) %all-gather.6.cloned.1.call-update) | async-done | bytes 9437200 | tf_op jit(solution)/shard_map/all_gather | solution.py:103
  234.5 7.8 %gather_fusion = bf16[60,128,384]{2,1,0:T(8,128)(2,1)} fusion(bf16[96,128,384]{2,1,0:T(8,128)(2,1)} %all-gather.6.cloned.1.call-done, s32[1024]{0:T(1024)S(1)} %pad_clamp_fusion.1), kind=kCustom, calls=%fused_computation | custom fusion | bytes 11796720 | tf_op jit(solution)/shard_map/gather | solution.py:106
  242.3 15.8 %reshape.242 = bf16[6,1280,3,128]{3,2,1,0:T(4,128)(2,1)} reshape(bf16[60,128,384]{2,1,0:T(8,128)(2,1)} %gather_fusion) | data formatting | bytes 11796480 | tf_op jit(solution)/shard_map/reshape | solution.py:106
  258.2 9.2 %fusion.19 = bf16[6,128,3,128]{1,3,2,0:T(8,128)(2,1)S(1)} fusion(f32[6,3,128,1280]{3,2,1,0:T(8,128)} %get-tuple-element.24, f32[6,3,128]{2,1,0:T(4,128)S(1)} %get-tuple-element.23, bf16[6,1280,3,128]{3,2,1,0:T(4,128)(2,1)} %reshape.242), kind=kOutput, calls=%fused_computation.21 | convolution fusion | flops 761167872 | bytes 18293760 | tf_op jit(solution)/shard_map/nhqk,nkhd->nqhd/dot_general | solution.py:116
  267.8 8.8 %convolution_convert_fusion = bf16[768,5120]{1,0:T(8,128)(2,1)} fusion(bf16[384,5120]{1,0:T(8,128)(2,1)} %param.15, bf16[48,8,6,128]{3,2,1,0:T(8,128)(2,1)S(1)} %bitcast.62), kind=kOutput, calls=%fused_computation.11 | convolution fusion | flops 3023831040 | bytes 12386304 | tf_op jit(solution)/shard_map/dot_general | solution.py:126
  276.6 10.6 %copy.54 = bf16[768,5120]{0,1:T(8,128)(2,1)} copy(bf16[768,5120]{1,0:T(8,128)(2,1)} %convolution_convert_fusion) | data formatting | bytes 15728640
  288.9 49.6 %reduce-scatter.4.cloned.1.call-done = bf16[640,768]{1,0:T(8,128)(2,1)} async-done(((bf16[5120,768]{1,0:T(8,128)(2,1)}), bf16[640,768]{1,0:T(8,128)(2,1)}) %reduce-scatter.4.cloned.1.call-update) | async-done | bytes 983056
  338.6 1.5 copy.55
  340.1 58.1 %all-reduce.2.cloned.1.call-done = bf16[768,64]{0,1:T(8,128)(2,1)} async-done(((bf16[768,64]{0,1:T(8,128)(2,1)}), bf16[768,64]{0,1:T(8,128)(2,1)}) %all-reduce.2.cloned.1.call-update) | async-done | bytes 98320 | tf_op jit(solution)/shard_map/psum | solution.py:120
  398.2 2.3 add_convert_fusion
  (57 shorter events, 10.5 us)
Async XLA Ops:
  6.5 52.4 %copy-start = (bf16[5120,192]{0,1:T(8,128)(2,1)S(1)}, bf16[5120,192]{0,1:T(8,128)(2,1)}, u32[]{:S(2)}) copy-start(bf16[5120,192]{0,1:T(8,128)(2,1)} %param.13) | copy-start | bytes 5898244
  6.5 52.4 %all-gather.4.cloned.1.call-start = ((), (), s32[]{:S(2)}) async-start(), calls=%async_computation.1 | async-start | bytes 8847360 | tf_op jit(solution)/shard_map/all_gather | solution.py:73
  7.3 150.0 %all-gather.8.cloned.1.call-start = ((), (), s32[]{:S(2)}) async-start(), calls=%async_computation.3 | async-start | bytes 10027008 | tf_op jit(solution)/shard_map/all_gather | solution.py:102
  27.5 37.5 %copy-start.4 = (bf16[64,3,384]{2,0,1:T(8,128)(2,1)S(1)}, bf16[64,3,384]{2,0,1:T(8,128)(2,1)}, u32[]{:S(2)}) copy-start(bf16[64,3,384]{2,0,1:T(8,128)(2,1)} %param.14) | copy-start | bytes 442372
  58.9 6.8 %copy-start.2 = (bf16[5120,3,384]{0,2,1:T(8,128)(2,1)S(1)}, bf16[5120,3,384]{0,2,1:T(8,128)(2,1)}, u32[]{:S(2)}) copy-start(bf16[5120,3,384]{0,2,1:T(8,128)(2,1)} %copy.37) | copy-start | bytes 35389444
  79.0 1.7 copy-start.3
  79.2 6.4 %copy-start.7 = (s32[96,10]{0,1:T(8,128)S(1)}, s32[96,10]{0,1:T(8,128)}, u32[]{:S(2)}) copy-start(s32[96,10]{0,1:T(8,128)} %param.11) | copy-start | bytes 11524
  82.9 151.7 %all-gather.6.cloned.1.call-start = ((), (), s32[]{:S(2)}) async-start(), calls=%async_computation.2 | async-start | bytes 10027008 | tf_op jit(solution)/shard_map/all_gather | solution.py:103
  85.3 253.2 %reduce-scatter.4.cloned.1.call-start = ((), (), s32[]{:S(2)}) async-start(), calls=%async_computation.5 | async-start | bytes 8847360
  287.2 0.8 copy-start.6
  287.2 111.0 %copy-start.5 = (bf16[64,640]{1,0:T(8,128)(2,1)S(1)}, bf16[64,640]{1,0:T(8,128)(2,1)}, u32[]{:S(2)}) copy-start(bf16[64,640]{1,0:T(8,128)(2,1)} %param.17) | copy-start | bytes 245764
  287.2 113.3 %copy-start.1 = (bf16[5120,192]{0,1:T(8,128)(2,1)S(1)}, bf16[5120,192]{0,1:T(8,128)(2,1)}, u32[]{:S(2)}) copy-start(bf16[5120,192]{0,1:T(8,128)(2,1)} %param.13) | copy-start | bytes 5898244
  287.3 111.0 %all-reduce.2.cloned.1.call-start = ((), (), s32[]{:S(2)}) async-start(), calls=%async_computation.4 | async-start | bytes 196608 | tf_op jit(solution)/shard_map/psum | solution.py:120
Sparse Core Ops, SparseCore 0:
  9.0 49.8 all-gather.3
  83.0 74.1 all-gather.7
  159.4 75.1 all-gather.5
  287.4 51.1 reduce-scatter.3
  340.8 57.4 all-reduce.1
where the time goes:
time: 409 us; the launch traced here: 407 us
  waiting for transfers between devices  238 us (58%)
  local copies, waits for them, and re-layouts  86.9 us (21%)
  matrix products  50.6 us (12%)
  other arithmetic  18.3 us (4%)
  between operations  13.4 us (3%)
    all_gather x1, waiting for transfers between devices, body(): lax.all_gather(key_tiles, 'frame', axis=0, tiled=True)  69 us
    psum x1, waiting for transfers between devices, body(): lax.psum(jnp.dot(attention_result, output_down_weight, preferred_element_...  58.1 us
    unnamed x6, waiting for transfers between devices  50.4 us
    all_gather x1, waiting for transfers between devices, body(): rank_segment = lax.all_gather(tokens, 'head', axis=1, tiled=True)  31.4 us
    unnamed x19, local copies, waits for them, and re-layouts  30.2 us
    all_gather x1, waiting for transfers between devices, body(): lax.all_gather(value_tiles, 'frame', axis=0, tiled=True)  28.7 us
    reshape x1, local copies, waits for them, and re-layouts, body(): pool_keys[my_lists]  15.9 us
    reshape x1, local copies, waits for them, and re-layouts, body(): pool_values[my_lists]  15.8 us
  transfers between devices with their start and end apart: 5, of which 5 were waited for; matrix products, arithmetic and copies ran while one was open for 19% of the time, Pallas kernels for 0%

commit v1 on v0

v1 whole, which is shorter than its diff:
```python
import functools
import math

import jax
import jax.numpy as jnp
import numpy as np
from jax import lax
from jax.experimental import pallas as pl
from jax.experimental.pallas import tpu as pltpu
from jax.sharding import PartitionSpec as P

MODEL_WIDTH = 5120
HEAD_SIZE = 128
BLOCK = 128
LISTED = 10
NBLK = 6
GROUPS = 16
NB = 96
RANK = 64
HEADS = 3
SHARD = 640
TIME_PAIRS = 22
SPACE_PAIRS = 42
MESH = pl.DeviceIdType.MESH
F32 = jnp.float32
BF16 = jnp.bfloat16

OFFSETS = ((1, 0, 4), (-1, 4, 4), (2, 8, 2), (-2, 10, 2), (3, 12, 1), (-3, 13, 1), (8, 14, 2))
SLOTS = 16


def rope_constants():
    lanes = np.zeros((8, 128), np.float64)
    t = 10000.0 ** (-np.arange(TIME_PAIRS) / TIME_PAIRS)
    s = 10000.0 ** (-np.arange(SPACE_PAIRS) / SPACE_PAIRS)
    lanes[0] = np.concatenate([t, t, s, s])
    lanes[1] = np.concatenate(
        [-np.ones(TIME_PAIRS), np.ones(TIME_PAIRS), -np.ones(SPACE_PAIRS), np.ones(SPACE_PAIRS)]
    )
    lanes[2, : 2 * TIME_PAIRS] = 1.0
    return lanes.astype(np.float32)


def sin_cos(x):
    turns = jnp.floor(x * (1.0 / (2.0 * math.pi)) + 0.5)
    c1 = 6.28125
    c2 = float(np.float32(np.round((2 * math.pi - c1) * 2**20) / 2**20))
    c3 = 2 * math.pi - c1 - c2
    r = ((x - turns * c1) - turns * c2) - turns * c3
    r2 = r * r
    s = jnp.full_like(r, -1.0 / math.factorial(19))
    for n in (17, 15, 13, 11, 9, 7, 5, 3, 1):
        s = s * r2 + (1.0 if n % 4 == 1 else -1.0) / math.factorial(n)
    c = jnp.full_like(r, 1.0 / math.factorial(20))
    for n in (18, 16, 14, 12, 10, 8, 6, 4, 2, 0):
        c = c * r2 + (1.0 if n % 4 == 0 else -1.0) / math.factorial(n)
    return s * r, c


def kernel(
    tok, tabv, tabs, mbf, consts, wq, dn, up,
    out,
    xg, wv, dnv, upv, cosv, sinv, planv, plans, acc, accl, qv, own, sb, pool0, pool1, pool2, sc,
    loc_sem, ag_send, ag_recv, kv_send, kv_recv, plan_sem,
):
    f = lax.axis_index("frame")
    h = lax.axis_index("head")
    z = h // 2
    core = h % 2
    up_h = ((z + 1) % 4) * 2 + core
    dn_h = ((z + 3) % 4) * 2 + core
    far_h = ((z + 2) % 4) * 2 + core
    other = z * 2 + (1 - core)
    f8 = (f + 8) % GROUPS
    pools = (pool0, pool1, pool2)

    def target(d):
        if d == 8:
            return f8, None
        dst = f + d
        return dst, (dst >= 0) & (dst < GROUPS)

    rows_all = pl.ds(0, NBLK * BLOCK)
    ld_tok = pltpu.make_async_copy(
        tok, xg.at[rows_all, pl.ds(pl.multiple_of(h * SHARD, 128), SHARD)], loc_sem.at[0]
    )
    ld_w = pltpu.make_async_copy(wq, wv, loc_sem.at[1])
    ld_dn = pltpu.make_async_copy(dn, dnv, loc_sem.at[2])
    ld_tok.start()
    ld_w.start()
    ld_dn.start()

    barrier = pltpu.get_barrier_semaphore()
    for hh in (up_h, dn_h, other):
        pl.semaphore_signal(barrier, inc=1, device_id=(f, hh), device_id_type=MESH)
    for d, _, _ in OFFSETS:
        dst, ok = target(d)

        def greet(dst=dst):
            pl.semaphore_signal(barrier, inc=1, device_id=(dst, h), device_id_type=MESH)

        if ok is None:
            greet()
        else:
            pl.when(ok)(greet)
    count = 4
    for d in (1, -1, 2, -2, 3, -3):
        count = count + ((f + d >= 0) & (f + d < GROUPS)).astype(jnp.int32)
    pl.semaphore_wait(barrier, count)

    def cols(hh):
        return pl.ds(pl.multiple_of(hh * SHARD, 128), SHARD)

    def rows(r, start=0, size=BLOCK):
        return pl.ds(pl.multiple_of(r * BLOCK + start, 64), size)

    def ag_copy(kind, r, src_h, dst_h, start=0, size=BLOCK, from_tok=False):
        dst = xg.at[rows(r, start, size), cols(src_h)]
        src = tok.at[rows(r, start, size), :] if from_tok else dst
        return pltpu.make_async_remote_copy(
            src_ref=src, dst_ref=dst, send_sem=ag_send.at[kind, r], recv_sem=ag_recv.at[kind, r],
            device_id=(f, dst_h), device_id_type=MESH,
        )

    HALF = BLOCK // 2
    def own_up(r):
        return ag_copy(0, r, h, up_h, from_tok=True)

    def own_dn(r):
        return ag_copy(1, r, h, dn_h, from_tok=True)

    def own_other(r):
        return ag_copy(2, r, h, other, from_tok=True)

    def relay_up(r):
        return ag_copy(3, r, dn_h, up_h, 0, HALF)

    def relay_dn(r):
        return ag_copy(4, r, up_h, dn_h, HALF, HALF)

    def share_dn(r):
        return ag_copy(5, r, dn_h, other)

    def share_up(r):
        return ag_copy(6, r, up_h, other)

    def share_far0(r):
        return ag_copy(7, r, far_h, other, 0, HALF)

    def share_far1(r):
        return ag_copy(8, r, far_h, other, HALF, HALF)

    def start_own(r):
        own_up(r).start()
        own_dn(r).start()
        own_other(r).start()

    start_own(0)
    start_own(1)

    tab = tabv[...]
    gi = lax.broadcasted_iota(jnp.int32, (NB, NB), 0)
    ri = lax.broadcasted_iota(jnp.int32, (NB, NB), 1)
    member = jnp.zeros((NB, NB), F32)
    for k in range(LISTED):
        member = jnp.maximum(member, (jnp.broadcast_to(tab[k : k + 1, :], (NB, NB)) == gi).astype(F32))
    rq = lax.broadcasted_iota(jnp.int32, (NB, 128), 0)
    qq = lax.broadcasted_iota(jnp.int32, (NB, 128), 1)
    in_group = ((rq * 43) >> 8 == qq).astype(F32)
    used = (jnp.dot(member, in_group, preferred_element_type=F32) > 0.5).astype(F32)
    lower = (((gi * 43) >> 8 == (ri * 43) >> 8) & (ri < gi)).astype(F32)
    rank = jnp.dot(lower, used, preferred_element_type=F32)
    code = jnp.where(used > 0.5, rank, -1.0)
    mine = jnp.sum(jnp.where(qq == f, rank, 0.0), axis=1, keepdims=True)
    delta = ((rq * 43) >> 8) - f
    base = jnp.zeros((NB, 128), F32)
    for d, slot, _ in OFFSETS:
        hit = (delta == -d) if d != 8 else ((delta == 8) | (delta == -8))
        base = jnp.where(hit, float(NBLK + slot), base)
    place = jnp.where(delta == 0, (rq - NBLK * f).astype(F32), base + mine)
    planv[...] = jnp.where(qq == 127, place, code).astype(jnp.int32)
    plan_cp = pltpu.make_async_copy(planv, plans, plan_sem)
    plan_cp.start()

    freq = consts[0:1, :]
    sign = consts[1:2, :]
    timed = consts[2:3, :] > 0.5
    inner = lax.broadcasted_iota(jnp.int32, (BLOCK, 128), 0)

    def table(b, carry):
        g = f * NBLK + b
        fr = mbf[g]

        def tally(i, n):
            return n + (mbf[i] < fr).astype(jnp.int32)

        first = lax.fori_loop(0, NB, tally, jnp.int32(0))
        pos = ((g - first) * BLOCK + inner).astype(F32)
        frame_pos = jnp.zeros((BLOCK, 128), F32) + fr.astype(F32)
        angle = jnp.where(jnp.broadcast_to(timed, (BLOCK, 128)), frame_pos, pos) * freq
        sn, cs = sin_cos(angle)
        cosv[rows(b), :] = cs
        sinv[rows(b), :] = sn * sign
        return carry

    lax.fori_loop(0, NBLK, table, 0)

    upv[...] = jnp.zeros_like(upv)
    for s in range(3):
        upv[s, s * RANK : (s + 1) * RANK, :] = up[s]

    ld_tok.wait()
    ld_w.wait()
    ld_dn.wait()
    plan_cp.wait()

    lane = lax.broadcasted_iota(jnp.int32, (BLOCK, 128), 1)

    def rope(u, cs, sn):
        rot = jnp.where(
            lane < TIME_PAIRS,
            pltpu.roll(u, 128 - TIME_PAIRS, 1),
            jnp.where(
                lane < 2 * TIME_PAIRS,
                pltpu.roll(u, TIME_PAIRS, 1),
                jnp.where(
                    lane < 2 * TIME_PAIRS + SPACE_PAIRS,
                    pltpu.roll(u, 128 - SPACE_PAIRS, 1),
                    pltpu.roll(u, SPACE_PAIRS, 1),
                ),
            ),
        )
        return u * cs + rot * sn

    KC = 1280

    def compute(r):
        def step(k, carry):
            ks = pl.ds(pl.multiple_of(k * KC, 128), KC)
            xk = xg[rows(r), ks]
            keep = (k > 0).astype(F32)
            for s in range(3):
                part = jnp.dot(xk, wv[s, ks, :], preferred_element_type=F32)
                acc[s] = jnp.where(k > 0, acc[s], 0.0) + part
            low = lax.dot_general(xk, dnv[:, ks], (((1,), (1,)), ((), ())), preferred_element_type=F32)
            accl[...] = jnp.where(k > 0, accl[...], 0.0) + low
            return carry

        lax.fori_loop(0, MODEL_WIDTH // KC, step, 0)
        low = accl[...].astype(BF16)
        cs = cosv[rows(r), :]
        sn = sinv[rows(r), :]
        for s in range(3):
            y = acc[s] + jnp.dot(low, upv[s], preferred_element_type=F32)
            for a in range(HEADS):
                u = y[:, a * 128 : (a + 1) * 128]
                if s == 0:
                    qv[a, rows(r), :] = rope(u, cs, sn).astype(BF16)
                elif s == 1:
                    k = rope(u, cs, sn).astype(BF16)
                    own[a, r, 0] = k
                    pools[a][r, 0] = k
                else:
                    v = u.astype(BF16)
                    own[a, r, 1] = v
                    pools[a][r, 1] = v

    def kv_copy(a, slot, dst):
        return pltpu.make_async_remote_copy(
            src_ref=sb.at[a, slot], dst_ref=pools[a].at[NBLK + slot],
            send_sem=kv_send.at[a, slot], recv_sem=kv_recv.at[a, slot],
            device_id=(dst, h), device_id_type=MESH,
        )

    def send_slot(d, slot, rank_of):
        dst, ok = target(d)

        def go():
            idx = jnp.int32(0)
            for b in range(1, NBLK):
                idx = jnp.where(plans[f * NBLK + b, dst] == rank_of, b, idx)
            for a in range(HEADS):
                sb[a, slot] = own[a, idx]
                kv_copy(a, slot, dst).start()

        if ok is None:
            go()
        else:
            pl.when(ok)(go)

    def finish(r):
        relay_up(r).wait_recv()
        share_far0(r).start()
        relay_dn(r).wait_recv()
        share_far1(r).start()
        own_other(r).wait_recv()
        share_dn(r).wait_recv()
        share_up(r).wait_recv()
        share_far0(r).wait_recv()
        share_far1(r).wait_recv()
        compute(r)
        for ready in range(NBLK):
            slots = [
                (d, first + i, i)
                for d, first, n in OFFSETS
                for i in range(n)
                if NBLK - n + i == ready
            ]
            if slots:

                @pl.when(r == ready)
                def _():
                    for d, slot, i in slots:
                        send_slot(d, slot, i)

    def ring(r, carry):
        own_up(r).wait_recv()
        relay_up(r).start()
        share_dn(r).start()
        own_dn(r).wait_recv()
        relay_dn(r).start()
        share_up(r).start()

        @pl.when(r + 2 < NBLK)
        def _():
            start_own(r + 2)

        @pl.when(r > 0)
        def _():
            finish(r - 1)

        return carry

    lax.fori_loop(0, NBLK, ring, 0)
    finish(NBLK - 1)

    def drain(r, carry):
        for cp in (own_up, own_dn, own_other, relay_up, relay_dn, share_dn, share_up, share_far0, share_far1):
            cp(r).wait_send()
        return carry

    scale = math.log2(math.e) / math.sqrt(HEAD_SIZE)

    def attend(a, b, carry):
        pool = pools[a]
        q = qv[a, rows(b), :]
        idx = [
            jnp.clip(plans[tabs[k, f * NBLK + b], 127], 0, NBLK + SLOTS - 1) for k in range(LISTED)
        ]
        top = None
        for k in range(0, LISTED, 2):
            kk = jnp.concatenate([pool[idx[k], 0], pool[idx[k + 1], 0]], axis=0)
            s = lax.dot_general(q, kk, (((1,), (1,)), ((), ())), preferred_element_type=F32)
            sc[:, k * 128 : (k + 2) * 128] = s
            part = jnp.maximum(s[:, :128], s[:, 128:])
            top = part if top is None else jnp.maximum(top, part)
        m = jnp.max(top, axis=1, keepdims=True)
        total = None
        o = None
        for k in range(0, LISTED, 2):
            p = jnp.exp2((sc[:, k * 128 : (k + 2) * 128] - m) * scale)
            t = p[:, :128] + p[:, 128:]
            total = t if total is None else total + t
            vv = jnp.concatenate([pool[idx[k], 1], pool[idx[k + 1], 1]], axis=0)
            po = jnp.dot(p.astype(BF16), vv, preferred_element_type=F32)
            o = po if o is None else o + po
        l = jnp.sum(total, axis=1, keepdims=True)
        out[rows(b), a * 128 : (a + 1) * 128] = (o / l).astype(BF16)
        return carry

    for a in range(HEADS):
        for d, first, n in OFFSETS:
            src = f8 if d == 8 else f - d

            def arrive(first=first, n=n, a=a):
                for i in range(n):
                    kv_copy(a, first + i, f8).wait_recv()

            if d == 8:
                arrive()
            else:
                pl.when((src >= 0) & (src < GROUPS))(arrive)
        lax.fori_loop(0, NBLK, functools.partial(attend, a), 0)

    lax.fori_loop(0, NBLK, drain, 0)
    for a in range(HEADS):
        for d, first, n in OFFSETS:
            dst, ok = target(d)

            def sent(first=first, n=n, a=a, dst=dst):
                for i in range(n):
                    kv_copy(a, first + i, f8).wait_send()

            if ok is None:
                sent()
            else:
                pl.when(ok)(sent)


def body(
    tokens,
    mask_block_frame,
    attended_key_blocks,
    frozen_query_key_value,
    query_key_value_down_weight,
    query_key_value_up_weight,
    frozen_output_weight,
    output_down_weight,
    output_up_weight,
):
    rows = tokens.shape[0]
    width = frozen_output_weight.shape[0]
    table = attended_key_blocks.T
    any_spec = pl.BlockSpec(memory_space=pl.ANY)
    vmem = pl.BlockSpec(memory_space=pltpu.VMEM)
    smem = pl.BlockSpec(memory_space=pltpu.SMEM)
    attention_result = pl.pallas_call(
        kernel,
        out_shape=jax.ShapeDtypeStruct((rows, width), BF16),
        in_specs=[any_spec, vmem, smem, smem, vmem, any_spec, any_spec, vmem],
        out_specs=vmem,
        scratch_shapes=[
            pltpu.VMEM((rows, MODEL_WIDTH), BF16),
            pltpu.VMEM((3, MODEL_WIDTH, width), BF16),
            pltpu.VMEM((3 * RANK, MODEL_WIDTH), BF16),
            pltpu.VMEM((3, 3 * RANK, width), BF16),
            pltpu.VMEM((rows, 128), F32),
            pltpu.VMEM((rows, 128), F32),
            pltpu.VMEM((NB, 128), jnp.int32),
            pltpu.SMEM((NB, 128), jnp.int32),
            pltpu.VMEM((3, BLOCK, width), F32),
            pltpu.VMEM((BLOCK, 3 * RANK), F32),
            pltpu.VMEM((HEADS, rows, 128), BF16),
            pltpu.VMEM((HEADS, NBLK, 2, BLOCK, 128), BF16),
            pltpu.VMEM((HEADS, SLOTS, 2, BLOCK, 128), BF16),
            pltpu.VMEM((NBLK + SLOTS, 2, BLOCK, 128), BF16),
            pltpu.VMEM((NBLK + SLOTS, 2, BLOCK, 128), BF16),
            pltpu.VMEM((NBLK + SLOTS, 2, BLOCK, 128), BF16),
            pltpu.VMEM((BLOCK, LISTED * BLOCK), F32),
            pltpu.SemaphoreType.DMA((3,)),
            pltpu.SemaphoreType.DMA((9, NBLK)),
            pltpu.SemaphoreType.DMA((9, NBLK)),
            pltpu.SemaphoreType.DMA((HEADS, SLOTS)),
            pltpu.SemaphoreType.DMA((HEADS, SLOTS)),
            pltpu.SemaphoreType.DMA,
        ],
        compiler_params=pltpu.CompilerParams(
            collective_id=0, has_side_effects=True, vmem_limit_bytes=62 * 1024 * 1024
        ),
    )(
        tokens,
        table,
        table,
        mask_block_frame,
        jnp.asarray(rope_constants()),
        frozen_query_key_value.transpose(1, 0, 2),
        query_key_value_down_weight.T,
        query_key_value_up_weight.transpose(1, 0, 2),
    )
    adapter_output = lax.psum(
        jnp.dot(attention_result, output_down_weight, preferred_element_type=F32).astype(BF16),
        "head",
    )
    partial_value = jnp.dot(attention_result, frozen_output_weight, preferred_element_type=F32)
    frozen_output = lax.psum_scatter(
        partial_value.astype(BF16), "head", scatter_dimension=1, tiled=True
    ).astype(F32)
    return (
        frozen_output + jnp.dot(adapter_output, output_up_weight, preferred_element_type=F32)
    ).astype(BF16)


def solution(mesh):
    return jax.shard_map(
        body,
        mesh=mesh,
        in_specs=(
            P("frame", "head"),
            P(),
            P(),
            P(None, None, "head"),
            P(),
            P(None, None, "head"),
            P("head", None),
            P("head", None),
            P(None, "head"),
        ),
        out_specs=P("frame", "head"),
        check_vma=False,
    )
```

time: 409 us -> 240 us (0.59)
  waiting for transfers between devices: 238 us -> 110 us
  Pallas kernels: 0 us -> 90.5 us
  local copies, waits for them, and re-layouts: 86.9 us -> 13.2 us
  matrix products: 50.6 us -> 12.9 us
  other arithmetic: 18.3 us -> 0 us
    all_gather x3 -> x0, waiting for transfers between devices: 129 us -> none  [the longest x1 69 us: body(): lax.all_gather(key_tiles, 'frame', axis=0, tiled=True)]
    pallas_call x0 -> x1, Pallas kernels: none -> 90.5 us  [body(): pl.pallas_call(kernel, out_shape=jax.ShapeDtypeStruct((rows, width), BF16...]
    dot_general x8 -> x3, matrix products: 50.6 us -> 12.9 us  [the longest x1 9.7 us: body(): jnp.dot(attention_result, frozen_output_weight, preferred_element_type=F32)]
    reshape x2 -> x0, local copies, waits for them, and re-layouts: 31.7 us -> none  [the longest x1 15.9 us: body(): pool_keys[my_lists]]
    gather x4 -> x0, local copies, waits for them, and re-layouts: 17.5 us -> none  [the longest x1 7.8 us: body(): pool_values[my_lists]]
    unnamed x19 -> x8, local copies, waits for them, and re-layouts: 30.2 us -> 13.2 us
    sub x1 -> x0, other arithmetic: 15.6 us -> none  [body(): powers = jnp.exp(scores - row_max)]
    unnamed x6 -> x3, waiting for transfers between devices: 50.4 us -> 48.8 us
  transfers between devices with their start and end apart: 5 -> 2, of which waited for: 5 -> 2; matrix products, arithmetic and copies ran while one was open for 19% -> 1% of each run, Pallas kernels for 0% -> 0%
where the time goes in v1:
time: 240 us
  waiting for transfers between devices  110 us (46%)
  Pallas kernels  90.5 us (38%)
  between operations  13.4 us (6%)
  local copies, waits for them, and re-layouts  13.2 us (6%)
  matrix products  12.9 us (5%)
    pallas_call x1, Pallas kernels, body(): pl.pallas_call(kernel, out_shape=jax.ShapeDtypeStruct((rows, width), BF16...  90.5 us
    psum x1, waiting for transfers between devices, body(): lax.psum(jnp.dot(attention_result, output_down_weight, preferred_element_...  60.8 us
    unnamed x3, waiting for transfers between devices  48.8 us
    unnamed x8, local copies, waits for them, and re-layouts  13.2 us
    dot_general x1, matrix products, body(): jnp.dot(attention_result, frozen_output_weight, preferred_element_type=F32)  9.7 us
  transfers between devices with their start and end apart: 2, of which 2 were waited for; matrix products, arithmetic and copies ran while one was open for 1% of the time, Pallas kernels for 0%

profile of v1, /device:TPU:14, one launch (start us, length us, event | category | flops | bytes accessed | tf_op | source)
XLA Modules:
  0.0 239.6 jit_solution(4089370608217253319)
XLA Ops:
  6.5 0.0 copy-start
  6.5 0.0 reduce-scatter.4.cloned.1.call-start
  6.5 90.5 %shard_map.100 = bf16[768,384]{1,0:T(8,128)(2,1)} custom-call(bf16[768,640]{1,0:T(8,128)(2,1)} %tok.1, s32[10,96]{1,0:T(8,128)} %bitcast.17, s32[10,96]{1,0:T(8,128)} %bitcast.18, s32[96]{0:T(128)} %mbf.1, f32[8,128]{1,0:T(8,128)} %constant.2.clone.consts, bf16[3,5120,384]{2,1,0:T(8,128)(2,1)} %bitcast.13, bf16[192,5120]{1,0:T(8,128)(2,1)} %bitcast.14, ...), custom_call_target="tpu_custom_call" | custom-call | tf_op jit(solution)/shard_map/pallas_call | solution.py:417
  97.0 9.7 %convolution_convert_fusion = bf16[768,5120]{1,0:T(8,128)(2,1)} fusion(bf16[768,384]{1,0:T(8,128)(2,1)} %shard_map.100, bf16[384,5120]{1,0:T(8,128)(2,1)} %param.16), kind=kOutput, calls=%fused_computation | convolution fusion | flops 3023831040 | bytes 12386304 | tf_op jit(solution)/shard_map/dot_general | solution.py:464
  106.7 10.6 %copy.11 = bf16[768,5120]{0,1:T(8,128)(2,1)} copy(bf16[768,5120]{1,0:T(8,128)(2,1)} %convolution_convert_fusion) | data formatting | bytes 15728640
  117.3 0.0 copy-start.1
  117.3 0.0 copy-start.2
  117.3 0.0 reduce-scatter.4.cloned.1.call-update
  117.4 0.0 all-reduce.2.cloned.1.call-start
  117.4 1.0 copy-done.1
  118.4 0.0 copy-done.2
  118.4 1.0 convolution_convert_fusion.1
  119.4 0.0 all-reduce.2.cloned.1.call-update
  119.4 48.7 %reduce-scatter.4.cloned.1.call-done = bf16[640,768]{1,0:T(8,128)(2,1)} async-done(((bf16[5120,768]{1,0:T(8,128)(2,1)}), bf16[640,768]{1,0:T(8,128)(2,1)}) %reduce-scatter.4.cloned.1.call-update) | async-done | bytes 983056
  168.1 1.5 copy.12
  169.7 60.8 %all-reduce.2.cloned.1.call-done = bf16[768,64]{1,0:T(8,128)(2,1)} async-done(((bf16[768,64]{1,0:T(8,128)(2,1)}), bf16[768,64]{1,0:T(8,128)(2,1)}) %all-reduce.2.cloned.1.call-update) | async-done | bytes 98320 | tf_op jit(solution)/shard_map/psum | solution.py:460
  230.5 0.0 copy-done
  230.5 2.3 add_convert_fusion
Async XLA Ops:
  6.5 223.9 %copy-start = (bf16[64,640]{1,0:T(8,128)(2,1)S(1)}, bf16[64,640]{1,0:T(8,128)(2,1)}, u32[]{:S(2)}) copy-start(bf16[64,640]{1,0:T(8,128)(2,1)} %param.18) | copy-start | bytes 245764
  6.5 161.6 %reduce-scatter.4.cloned.1.call-start = ((), (), s32[]{:S(2)}) async-start(), calls=%async_computation.2 | async-start | bytes 8847360
  117.3 1.1 copy-start.1
  117.3 1.1 copy-start.2
  117.4 113.1 %all-reduce.2.cloned.1.call-start = ((), (), s32[]{:S(2)}) async-start(), calls=%async_computation.1 | async-start | bytes 393216 | tf_op jit(solution)/shard_map/psum | solution.py:460
Sparse Core Ops, SparseCore 0:
  117.5 50.6 reduce-scatter.3
  170.4 59.9 all-reduce.1

commit v2 on v1

--- a/solution.py
+++ b/solution.py
@@ -21,6 +21,7 @@
 SHARD = 640
 TIME_PAIRS = 22
 SPACE_PAIRS = 42
+N_HEAD = 8
 MESH = pl.DeviceIdType.MESH
 F32 = jnp.float32
 BF16 = jnp.bfloat16
@@ -58,10 +59,12 @@
 
 
 def kernel(
-    tok, tabv, tabs, mbf, consts, wq, dn, up,
-    out,
+    tok, tabv, tabs, mbf, consts, wq, dn, up, wo, od, ou,
+    out, wog,
     xg, wv, dnv, upv, cosv, sinv, planv, plans, acc, accl, qv, own, sb, pool0, pool1, pool2, sc,
+    wov, odl, odg, attg, oacc, lacc,
     loc_sem, ag_send, ag_recv, kv_send, kv_recv, plan_sem,
+    wz_send, wz_recv, wr_send, wr_recv, at_send, at_recv,
 ):
     f = lax.axis_index("frame")
     h = lax.axis_index("head")
@@ -72,6 +75,12 @@
     far_h = ((z + 2) % 4) * 2 + core
     other = z * 2 + (1 - core)
     f8 = (f + 8) % GROUPS
+    y = f // 4
+    x = f % 4
+    x_up = y * 4 + (x + 1) % 4
+    x_dn = y * 4 + (x + 3) % 4
+    y_up = ((y + 1) % 4) * 4 + x
+    y_dn = ((y + 3) % 4) * 4 + x
     pools = (pool0, pool1, pool2)
 
     def target(d):
@@ -86,13 +95,21 @@
     )
     ld_w = pltpu.make_async_copy(wq, wv, loc_sem.at[1])
     ld_dn = pltpu.make_async_copy(dn, dnv, loc_sem.at[2])
+    ld_od = [
+        pltpu.make_async_copy(od.at[:, a * 128 : (a + 1) * 128], odl.at[a], loc_sem.at[3 + a])
+        for a in range(HEADS)
+    ]
     ld_tok.start()
+    for cp in ld_od:
+        cp.start()
     ld_w.start()
     ld_dn.start()
 
     barrier = pltpu.get_barrier_semaphore()
-    for hh in (up_h, dn_h, other):
-        pl.semaphore_signal(barrier, inc=1, device_id=(f, hh), device_id_type=MESH)
+    for j in range(1, N_HEAD):
+        pl.semaphore_signal(barrier, inc=1, device_id=(f, (h + j) % N_HEAD), device_id_type=MESH)
+    for ff in (x_up, x_dn, y_up, y_dn):
+        pl.semaphore_signal(barrier, inc=1, device_id=(ff, h), device_id_type=MESH)
     for d, _, _ in OFFSETS:
         dst, ok = target(d)
 
@@ -103,7 +120,7 @@
             greet()
         else:
             pl.when(ok)(greet)
-    count = 4
+    count = N_HEAD - 1 + 4 + 1
     for d in (1, -1, 2, -2, 3, -3):
         count = count + ((f + d >= 0) & (f + d < GROUPS)).astype(jnp.int32)
     pl.semaphore_wait(barrier, count)
@@ -122,6 +139,100 @@
             device_id=(f, dst_h), device_id_type=MESH,
         )
 
+    def wz_copy(j):
+        dst_h = (h + j) % N_HEAD
+        mine = jnp.where(h < 4, 4 * y + x, 4 * x + y)
+        part = pl.ds(pl.multiple_of(mine * 8, 8), 8)
+        src = wo.at[:, part, pl.ds(pl.multiple_of(dst_h * SHARD, 128), SHARD)]
+        dst = wog.at[:, h, part, :]
+        if j == 0:
+            return pltpu.make_async_copy(src, dst, wz_send.at[0])
+        return pltpu.make_async_remote_copy(
+            src_ref=src, dst_ref=dst, send_sem=wz_send.at[j], recv_sem=wz_recv.at[j],
+            device_id=(f, dst_h), device_id_type=MESH,
+        )
+
+    def ring_copy(half, stage, kind):
+        along_x = half == stage
+        here = x if along_x else y
+        fixed = y if along_x else x
+        if stage == 0:
+            size = 8
+            at = fixed * 4 + (here + 3) % 4 if kind == 2 else fixed * 4 + (here + 1) % 4 if kind == 3 else fixed * 4 + here
+        else:
+            size = 32
+            at = (here + 3) % 4 if kind == 2 else (here + 1) % 4 if kind == 3 else here
+        part = pl.ds(pl.multiple_of(at * size, 8), size)
+        lo = 4 * half + (2 if kind == 3 else 0)
+        n = 4 if kind < 2 else 2
+        ref = wog.at[:, lo : lo + n, part, :]
+        plus = kind in (0, 2)
+        dst = (x_up if plus else x_dn) if along_x else (y_up if plus else y_dn)
+        return pltpu.make_async_remote_copy(
+            src_ref=ref, dst_ref=ref, send_sem=wr_send.at[half * 2 + stage, kind],
+            recv_sem=wr_recv.at[half * 2 + stage, kind],
+            device_id=(dst, h), device_id_type=MESH,
+        )
+
+    def weights_step(i):
+        if i == 0:
+            wz_copy(0).wait()
+            for j in range(1, N_HEAD):
+                wz_copy(j).wait_recv()
+            for half in range(2):
+                ring_copy(half, 0, 0).start()
+                ring_copy(half, 0, 1).start()
+        elif i == 1 or i == 3:
+            for half in range(2):
+                for kind in range(2):
+                    ring_copy(half, i // 2, kind).wait_recv()
+                    ring_copy(half, i // 2, kind + 2).start()
+        else:
+            for half in range(2):
+                for kind in range(2, 4):
+                    ring_copy(half, i // 2 - 1, kind).wait_recv()
+            if i == 2:
+                for half in range(2):
+                    ring_copy(half, 1, 0).start()
+                    ring_copy(half, 1, 1).start()
+
+    def lanes(hh):
+        return pl.ds(pl.multiple_of(hh * 128, 128), 128)
+
+    def column_ring(view, i, src=None):
+        def cp(kind, src_h, dst_h, half=None):
+            dst = view(src_h, half)
+            return pltpu.make_async_remote_copy(
+                src_ref=src if src is not None and kind < 3 else dst, dst_ref=dst,
+                send_sem=at_send.at[kind, i], recv_sem=at_recv.at[kind, i],
+                device_id=(f, dst_h), device_id_type=MESH,
+            )
+
+        return (
+            cp(0, h, up_h), cp(1, h, dn_h), cp(2, h, other),
+            cp(3, dn_h, up_h, 0), cp(4, up_h, dn_h, 1),
+            cp(5, dn_h, other), cp(6, up_h, other),
+            cp(7, far_h, other, 0), cp(8, far_h, other, 1),
+        )
+
+    def advance(ring):
+        ring[0].wait_recv()
+        ring[3].start()
+        ring[5].start()
+        ring[1].wait_recv()
+        ring[4].start()
+        ring[6].start()
+
+    def spread(ring):
+        ring[3].wait_recv()
+        ring[7].start()
+        ring[4].wait_recv()
+        ring[8].start()
+
+    def settle(ring):
+        for i in (2, 5, 6, 7, 8):
+            ring[i].wait_recv()
+
     HALF = BLOCK // 2
     def own_up(r):
         return ag_copy(0, r, h, up_h, from_tok=True)
@@ -156,6 +267,8 @@
         own_other(r).start()
 
     start_own(0)
+    for j in range(N_HEAD):
+        wz_copy(j).start()
     start_own(1)
 
     tab = tabv[...]
@@ -325,6 +438,12 @@
         def _():
             start_own(r + 2)
 
+        for i in range(4):
+
+            @pl.when(r == i + 2)
+            def _():
+                weights_step(i)
+
         @pl.when(r > 0)
         def _():
             finish(r - 1)
@@ -332,7 +451,20 @@
         return carry
 
     lax.fori_loop(0, NBLK, ring, 0)
+    od_ring = column_ring(
+        lambda hh, half: odg.at[:, slice(0, RANK) if half is None else slice(32 * half, 32 * half + 32), lanes(hh)],
+        NBLK, odl,
+    )
+    for cp in ld_od:
+        cp.wait()
+    for a in range(HEADS):
+        odg[a, :, lanes(h)] = odl[a]
+    for i in range(3):
+        od_ring[i].start()
     finish(NBLK - 1)
+    advance(od_ring)
+    spread(od_ring)
+    settle(od_ring)
 
     def drain(r, carry):
         for cp in (own_up, own_dn, own_other, relay_up, relay_dn, share_dn, share_up, share_far0, share_far1):
@@ -365,23 +497,93 @@
             po = jnp.dot(p.astype(BF16), vv, preferred_element_type=F32)
             o = po if o is None else o + po
         l = jnp.sum(total, axis=1, keepdims=True)
-        out[rows(b), a * 128 : (a + 1) * 128] = (o / l).astype(BF16)
+        attg[a, rows(b), lanes(h)] = (o / l).astype(BF16)
         return carry
 
-    for a in range(HEADS):
-        for d, first, n in OFFSETS:
-            src = f8 if d == 8 else f - d
-
-            def arrive(first=first, n=n, a=a):
-                for i in range(n):
-                    kv_copy(a, first + i, f8).wait_recv()
-
-            if d == 8:
-                arrive()
+    PART = 3 * BLOCK
+
+    def at_ring(i):
+        a, c = i // 2, i % 2
+
+        def view(hh, half):
+            start = c * PART + (0 if half is None else half * (PART // 2))
+            return attg.at[a, start : start + (PART if half is None else PART // 2), lanes(hh)]
+
+        return column_ring(view, i)
+
+    def project(i):
+        a, c = i // 2, i % 2
+
+        def go(b, carry):
+            xa = attg[a, rows(b), :]
+            part = jnp.dot(xa, wov[a].reshape(N_HEAD * 128, SHARD), preferred_element_type=F32)
+            low = lax.dot_general(xa, odg[a], (((1,), (1,)), ((), ())), preferred_element_type=F32)
+            if a == 0:
+                oacc[rows(b), :] = part
+                lacc[rows(b), :] = low
+            elif a == 1:
+                oacc[rows(b), :] += part
+                lacc[rows(b), :] += low
             else:
-                pl.when((src >= 0) & (src < GROUPS))(arrive)
-        lax.fori_loop(0, NBLK, functools.partial(attend, a), 0)
-
+                low = (lacc[rows(b), :] + low).astype(BF16)
+                total = oacc[rows(b), :] + part
+                out[rows(b), :] = (
+                    total + jnp.dot(low, ou[...], preferred_element_type=F32)
+                ).astype(BF16)
+            return carry
+
+        lax.fori_loop(c * 3, c * 3 + 3, go, 0)
+
+    ld_wo = pltpu.make_async_copy(wog, wov, loc_sem.at[6])
+    rings = [at_ring(i) for i in range(2 * HEADS)]
+    for i in range(2 * HEADS):
+        a, c = i // 2, i % 2
+        if c == 0:
+            for d, first, n in OFFSETS:
+                src = f8 if d == 8 else f - d
+
+                def arrive(first=first, n=n, a=a):
+                    for j in range(n):
+                        kv_copy(a, first + j, f8).wait_recv()
+
+                if d == 8:
+                    arrive()
+                else:
+                    pl.when((src >= 0) & (src < GROUPS))(arrive)
+        lax.fori_loop(c * 3, c * 3 + 3, functools.partial(attend, a), 0)
+        for j in range(3):
+            rings[i][j].start()
+        if i == 0:
+            weights_step(4)
+            ld_wo.start()
+        if i >= 1:
+            advance(rings[i - 1])
+        if i >= 2:
+            spread(rings[i - 2])
+        if i == 3:
+            ld_wo.wait()
+        if i >= 3:
+            settle(rings[i - 3])
+            project(i - 3)
+    advance(rings[5])
+    spread(rings[4])
+    settle(rings[3])
+    project(3)
+    spread(rings[5])
+    settle(rings[4])
+    project(4)
+    settle(rings[5])
+    project(5)
+
+    for ring in rings + [od_ring]:
+        for cp in ring:
+            cp.wait_send()
+    for j in range(1, N_HEAD):
+        wz_copy(j).wait_send()
+    for half in range(2):
+        for stage in range(2):
+            for kind in range(4):
+                ring_copy(half, stage, kind).wait_send()
     lax.fori_loop(0, NBLK, drain, 0)
     for a in range(HEADS):
         for d, first, n in OFFSETS:
@@ -414,11 +616,16 @@
     any_spec = pl.BlockSpec(memory_space=pl.ANY)
     vmem = pl.BlockSpec(memory_space=pltpu.VMEM)
     smem = pl.BlockSpec(memory_space=pltpu.SMEM)
-    attention_result = pl.pallas_call(
+    out, _ = pl.pallas_call(
         kernel,
-        out_shape=jax.ShapeDtypeStruct((rows, width), BF16),
-        in_specs=[any_spec, vmem, smem, smem, vmem, any_spec, any_spec, vmem],
-        out_specs=vmem,
+        out_shape=(
+            jax.ShapeDtypeStruct((rows, SHARD), BF16),
+            jax.ShapeDtypeStruct((HEADS, N_HEAD, 128, SHARD), BF16),
+        ),
+        in_specs=[
+            any_spec, vmem, smem, smem, vmem, any_spec, any_spec, vmem, any_spec, any_spec, vmem
+        ],
+        out_specs=(vmem, any_spec),
         scratch_shapes=[
             pltpu.VMEM((rows, MODEL_WIDTH), BF16),
             pltpu.VMEM((3, MODEL_WIDTH, width), BF16),
@@ -437,12 +644,24 @@
             pltpu.VMEM((NBLK + SLOTS, 2, BLOCK, 128), BF16),
             pltpu.VMEM((NBLK + SLOTS, 2, BLOCK, 128), BF16),
             pltpu.VMEM((BLOCK, LISTED * BLOCK), F32),
-            pltpu.SemaphoreType.DMA((3,)),
+            pltpu.VMEM((HEADS, N_HEAD, 128, SHARD), BF16),
+            pltpu.VMEM((HEADS, RANK, 128), BF16),
+            pltpu.VMEM((HEADS, RANK, N_HEAD * 128), BF16),
+            pltpu.VMEM((HEADS, rows, N_HEAD * 128), BF16),
+            pltpu.VMEM((rows, SHARD), F32),
+            pltpu.VMEM((rows, RANK), F32),
+            pltpu.SemaphoreType.DMA((7,)),
             pltpu.SemaphoreType.DMA((9, NBLK)),
             pltpu.SemaphoreType.DMA((9, NBLK)),
             pltpu.SemaphoreType.DMA((HEADS, SLOTS)),
             pltpu.SemaphoreType.DMA((HEADS, SLOTS)),
             pltpu.SemaphoreType.DMA,
+            pltpu.SemaphoreType.DMA((N_HEAD,)),
+            pltpu.SemaphoreType.DMA((N_HEAD,)),
+            pltpu.SemaphoreType.DMA((4, 4)),
+            pltpu.SemaphoreType.DMA((4, 4)),
+            pltpu.SemaphoreType.DMA((9, NBLK + 1)),
+            pltpu.SemaphoreType.DMA((9, NBLK + 1)),
         ],
         compiler_params=pltpu.CompilerParams(
             collective_id=0, has_side_effects=True, vmem_limit_bytes=62 * 1024 * 1024
@@ -456,18 +675,11 @@
         frozen_query_key_value.transpose(1, 0, 2),
         query_key_value_down_weight.T,
         query_key_value_up_weight.transpose(1, 0, 2),
+        frozen_output_weight.reshape(HEADS, 128, MODEL_WIDTH),
+        output_down_weight.T,
+        output_up_weight,
     )
-    adapter_output = lax.psum(
-        jnp.dot(attention_result, output_down_weight, preferred_element_type=F32).astype(BF16),
-        "head",
-    )
-    partial_value = jnp.dot(attention_result, frozen_output_weight, preferred_element_type=F32)
-    frozen_output = lax.psum_scatter(
-        partial_value.astype(BF16), "head", scatter_dimension=1, tiled=True
-    ).astype(F32)
-    return (
-        frozen_output + jnp.dot(adapter_output, output_up_weight, preferred_element_type=F32)
-    ).astype(BF16)
+    return out
 
 
 def solution(mesh):

time: 240 us -> 132 us (0.55)
  waiting for transfers between devices: 110 us -> 0 us
  Pallas kernels: 90.5 us -> 129 us
  between operations: 13.4 us -> 0.01 us
  matrix products: 12.9 us -> 0 us
  local copies, waits for them, and re-layouts: 13.2 us -> 2.23 us
    psum x1 -> x0, waiting for transfers between devices: 60.8 us -> none  [body(): lax.psum(jnp.dot(attention_result, output_down_weight, preferred_element_...]
    unnamed x3 -> x0, waiting for transfers between devices: 48.8 us -> none
    pallas_call x1, Pallas kernels: 90.5 us -> 129 us  [body(): pl.pallas_call(kernel, out_shape=(jax.ShapeDtypeStruct((rows, SHARD), BF1...]
    dot_general x3 -> x0, matrix products: 12.9 us -> none  [the longest x1 9.7 us: body(): jnp.dot(attention_result, frozen_output_weight, preferred_element_type=F32)]
    unnamed x8 -> x1, local copies, waits for them, and re-layouts: 13.2 us -> 2.23 us
  transfers between devices with their start and end apart: 2 -> 0, of which waited for: 2 -> 0; matrix products, arithmetic and copies ran while one was open for 1% -> 0% of each run, Pallas kernels for 0% -> 0%
where the time goes in v2:
time: 132 us; the launch traced here: 131 us
  Pallas kernels  129 us (98%)
  local copies, waits for them, and re-layouts  2.23 us (2%)
    pallas_call x1, Pallas kernels, body(): pl.pallas_call(kernel, out_shape=(jax.ShapeDtypeStruct((rows, SHARD), BF1...  129 us

profile of v2, /device:TPU:14, one launch (start us, length us, event | category | flops | bytes accessed | tf_op | source)
XLA Modules:
  0.0 131.4 jit_solution(3205318325606372135)
XLA Ops:
  0.0 129.1 %shard_map.100 = (bf16[768,640]{1,0:T(8,128)(2,1)}, bf16[3,8,128,640]{3,2,1,0:T(8,128)(2,1)}) custom-call(bf16[768,640]{1,0:T(8,128)(2,1)} %tok.1, s32[10,96]{1,0:T(8,128)} %bitcast.11, s32[10,96]{1,0:T(8,128)} %bitcast.12, s32[96]{0:T(128)} %mbf.1, f32[8,128]{1,0:T(8,128)} %constant.2.clone.consts, bf16[3,5120,384]{2,1,0:T(8,128)(2,1)} %bitcast.6, ...), custom_call_target="tpu_custom_call" | custom-call | tf_op jit(solution)/shard_map/pallas_call | solution.py:619
  129.1 2.2 %copy.12 = bf16[768,640]{1,0:T(8,128)(2,1)} copy(bf16[768,640]{1,0:T(8,128)(2,1)} %get-tuple-element.6) | data formatting | bytes 1966080

commit v3 on v2

--- a/solution.py
+++ b/solution.py
@@ -266,9 +266,9 @@
         own_dn(r).start()
         own_other(r).start()
 
-    start_own(0)
     for j in range(N_HEAD):
         wz_copy(j).start()
+    start_own(0)
     start_own(1)
 
     tab = tabv[...]
@@ -322,6 +322,7 @@
     for s in range(3):
         upv[s, s * RANK : (s + 1) * RANK, :] = up[s]
 
+    weights_step(0)
     ld_tok.wait()
     ld_w.wait()
     ld_dn.wait()
@@ -438,9 +439,9 @@
         def _():
             start_own(r + 2)
 
-        for i in range(4):
-
-            @pl.when(r == i + 2)
+        for i, at in ((1, 1), (2, 2), (3, 4)):
+
+            @pl.when(r == at)
             def _():
                 weights_step(i)
 

time: 132 us -> 122 us (0.924)
  Pallas kernels: 129 us -> 119 us
    pallas_call x1, Pallas kernels: 129 us -> 119 us  [body(): pl.pallas_call(kernel, out_shape=(jax.ShapeDtypeStruct((rows, SHARD), BF1...]
where the time goes in v3:
time: 122 us
  Pallas kernels  119 us (98%)
  local copies, waits for them, and re-layouts  2.23 us (2%)
    pallas_call x1, Pallas kernels, body(): pl.pallas_call(kernel, out_shape=(jax.ShapeDtypeStruct((rows, SHARD), BF1...  119 us

profile of v3, /device:TPU:14, one launch (start us, length us, event | category | flops | bytes accessed | tf_op | source)
XLA Modules:
  0.0 121.5 jit_solution(3168503826416500078)
XLA Ops:
  0.0 119.3 %shard_map.100 = (bf16[768,640]{1,0:T(8,128)(2,1)}, bf16[3,8,128,640]{3,2,1,0:T(8,128)(2,1)}) custom-call(bf16[768,640]{1,0:T(8,128)(2,1)} %tok.1, s32[10,96]{1,0:T(8,128)} %bitcast.11, s32[10,96]{1,0:T(8,128)} %bitcast.12, s32[96]{0:T(128)} %mbf.1, f32[8,128]{1,0:T(8,128)} %constant.2.clone.consts, bf16[3,5120,384]{2,1,0:T(8,128)(2,1)} %bitcast.6, ...), custom_call_target="tpu_custom_call" | custom-call | tf_op jit(solution)/shard_map/pallas_call | solution.py:620
  119.3 2.2 %copy.12 = bf16[768,640]{1,0:T(8,128)(2,1)} copy(bf16[768,640]{1,0:T(8,128)(2,1)} %get-tuple-element.6) | data formatting | bytes 1966080

commit v4 on v3

--- a/solution.py
+++ b/solution.py
@@ -386,21 +386,26 @@
             device_id=(dst, h), device_id_type=MESH,
         )
 
-    def send_slot(d, slot, rank_of):
-        dst, ok = target(d)
-
-        def go():
+    def send_slots(slots):
+        picks = []
+        for d, slot, rank_of in slots:
+            dst, ok = target(d)
+            col = dst if ok is None else jnp.clip(dst, 0, GROUPS - 1)
             idx = jnp.int32(0)
             for b in range(1, NBLK):
-                idx = jnp.where(plans[f * NBLK + b, dst] == rank_of, b, idx)
-            for a in range(HEADS):
-                sb[a, slot] = own[a, idx]
-                kv_copy(a, slot, dst).start()
-
-        if ok is None:
-            go()
-        else:
-            pl.when(ok)(go)
+                idx = jnp.where(plans[f * NBLK + b, col] == rank_of, b, idx)
+            picks.append((dst, ok, slot, idx))
+        for a in range(HEADS):
+            for dst, ok, slot, idx in picks:
+
+                def go(dst=dst, slot=slot, idx=idx, a=a):
+                    sb[a, slot] = own[a, idx]
+                    kv_copy(a, slot, dst).start()
+
+                if ok is None:
+                    go()
+                else:
+                    pl.when(ok)(go)
 
     def finish(r):
         relay_up(r).wait_recv()
@@ -424,8 +429,7 @@
 
                 @pl.when(r == ready)
                 def _():
-                    for d, slot, i in slots:
-                        send_slot(d, slot, i)
+                    send_slots(slots)
 
     def ring(r, carry):
         own_up(r).wait_recv()

time: 122 us -> 119 us (0.975)
  Pallas kernels: 119 us -> 116 us
    pallas_call x1, Pallas kernels: 119 us -> 116 us  [body(): pl.pallas_call(kernel, out_shape=(jax.ShapeDtypeStruct((rows, SHARD), BF1...]
where the time goes in v4:
time: 119 us; the launch traced here: 118 us
  Pallas kernels  116 us (97%)
  local copies, waits for them, and re-layouts  2.23 us (2%)
    pallas_call x1, Pallas kernels, body(): pl.pallas_call(kernel, out_shape=(jax.ShapeDtypeStruct((rows, SHARD), BF1...  116 us

profile of v4, /device:TPU:14, one launch (start us, length us, event | category | flops | bytes accessed | tf_op | source)
XLA Modules:
  0.0 117.9 jit_solution(14079009940702709599)
XLA Ops:
  0.0 115.6 %shard_map.100 = (bf16[768,640]{1,0:T(8,128)(2,1)}, bf16[3,8,128,640]{3,2,1,0:T(8,128)(2,1)}) custom-call(bf16[768,640]{1,0:T(8,128)(2,1)} %tok.1, s32[10,96]{1,0:T(8,128)} %bitcast.11, s32[10,96]{1,0:T(8,128)} %bitcast.12, s32[96]{0:T(128)} %mbf.1, f32[8,128]{1,0:T(8,128)} %constant.2.clone.consts, bf16[3,5120,384]{2,1,0:T(8,128)(2,1)} %bitcast.6, ...), custom_call_target="tpu_custom_call" | custom-call | tf_op jit(solution)/shard_map/pallas_call | solution.py:624
  115.6 2.2 %copy.12 = bf16[768,640]{1,0:T(8,128)(2,1)} copy(bf16[768,640]{1,0:T(8,128)(2,1)} %get-tuple-element.6) | data formatting | bytes 1966080

commit v5 on v4

--- a/solution.py
+++ b/solution.py
@@ -443,7 +443,7 @@
         def _():
             start_own(r + 2)
 
-        for i, at in ((1, 1), (2, 2), (3, 4)):
+        for i, at in ((1, 0), (2, 1), (3, 3)):
 
             @pl.when(r == at)
             def _():

time: 119 us -> 116 us (0.975)
  Pallas kernels: 116 us -> 113 us
    pallas_call x1, Pallas kernels: 116 us -> 113 us  [body(): pl.pallas_call(kernel, out_shape=(jax.ShapeDtypeStruct((rows, SHARD), BF1...]
where the time goes in v5:
time: 116 us; the launch traced here: 115 us
  Pallas kernels  113 us (97%)
  local copies, waits for them, and re-layouts  2.23 us (2%)
    pallas_call x1, Pallas kernels, body(): pl.pallas_call(kernel, out_shape=(jax.ShapeDtypeStruct((rows, SHARD), BF1...  113 us

profile of v5, /device:TPU:14, one launch (start us, length us, event | category | flops | bytes accessed | tf_op | source)
XLA Modules:
  0.0 115.1 jit_solution(13195453154299696763)
XLA Ops:
  0.0 112.9 %shard_map.100 = (bf16[768,640]{1,0:T(8,128)(2,1)}, bf16[3,8,128,640]{3,2,1,0:T(8,128)(2,1)}) custom-call(bf16[768,640]{1,0:T(8,128)(2,1)} %tok.1, s32[10,96]{1,0:T(8,128)} %bitcast.11, s32[10,96]{1,0:T(8,128)} %bitcast.12, s32[96]{0:T(128)} %mbf.1, f32[8,128]{1,0:T(8,128)} %constant.2.clone.consts, bf16[3,5120,384]{2,1,0:T(8,128)(2,1)} %bitcast.6, ...), custom_call_target="tpu_custom_call" | custom-call | tf_op jit(solution)/shard_map/pallas_call | solution.py:624
  112.9 2.2 %copy.12 = bf16[768,640]{1,0:T(8,128)(2,1)} copy(bf16[768,640]{1,0:T(8,128)(2,1)} %get-tuple-element.6) | data formatting | bytes 1966080

commit v6 on v5

--- a/solution.py
+++ b/solution.py
@@ -458,7 +458,7 @@
     lax.fori_loop(0, NBLK, ring, 0)
     od_ring = column_ring(
         lambda hh, half: odg.at[:, slice(0, RANK) if half is None else slice(32 * half, 32 * half + 32), lanes(hh)],
-        NBLK, odl,
+        3 * HEADS, odl,
     )
     for cp in ld_od:
         cp.wait()
@@ -505,10 +505,12 @@
         attg[a, rows(b), lanes(h)] = (o / l).astype(BF16)
         return carry
 
-    PART = 3 * BLOCK
+    PARTS = 3
+    PART = NBLK // PARTS * BLOCK
+    STEPS = NBLK // PARTS
 
     def at_ring(i):
-        a, c = i // 2, i % 2
+        a, c = i // PARTS, i % PARTS
 
         def view(hh, half):
             start = c * PART + (0 if half is None else half * (PART // 2))
@@ -517,7 +519,7 @@
         return column_ring(view, i)
 
     def project(i):
-        a, c = i // 2, i % 2
+        a, c = i // PARTS, i % PARTS
 
         def go(b, carry):
             xa = attg[a, rows(b), :]
@@ -537,12 +539,12 @@
                 ).astype(BF16)
             return carry
 
-        lax.fori_loop(c * 3, c * 3 + 3, go, 0)
+        lax.fori_loop(c * STEPS, (c + 1) * STEPS, go, 0)
 
     ld_wo = pltpu.make_async_copy(wog, wov, loc_sem.at[6])
-    rings = [at_ring(i) for i in range(2 * HEADS)]
-    for i in range(2 * HEADS):
-        a, c = i // 2, i % 2
+    rings = [at_ring(i) for i in range(PARTS * HEADS)]
+    for i in range(PARTS * HEADS):
+        a, c = i // PARTS, i % PARTS
         if c == 0:
             for d, first, n in OFFSETS:
                 src = f8 if d == 8 else f - d
@@ -555,7 +557,7 @@
                     arrive()
                 else:
                     pl.when((src >= 0) & (src < GROUPS))(arrive)
-        lax.fori_loop(c * 3, c * 3 + 3, functools.partial(attend, a), 0)
+        lax.fori_loop(c * STEPS, (c + 1) * STEPS, functools.partial(attend, a), 0)
         for j in range(3):
             rings[i][j].start()
         if i == 0:
@@ -570,15 +572,15 @@
         if i >= 3:
             settle(rings[i - 3])
             project(i - 3)
-    advance(rings[5])
-    spread(rings[4])
-    settle(rings[3])
-    project(3)
-    spread(rings[5])
-    settle(rings[4])
-    project(4)
-    settle(rings[5])
-    project(5)
+    advance(rings[8])
+    spread(rings[7])
+    settle(rings[6])
+    project(6)
+    spread(rings[8])
+    settle(rings[7])
+    project(7)
+    settle(rings[8])
+    project(8)
 
     for ring in rings + [od_ring]:
         for cp in ring:
@@ -665,8 +667,8 @@
             pltpu.SemaphoreType.DMA((N_HEAD,)),
             pltpu.SemaphoreType.DMA((4, 4)),
             pltpu.SemaphoreType.DMA((4, 4)),
-            pltpu.SemaphoreType.DMA((9, NBLK + 1)),
-            pltpu.SemaphoreType.DMA((9, NBLK + 1)),
+            pltpu.SemaphoreType.DMA((9, 3 * HEADS + 1)),
+            pltpu.SemaphoreType.DMA((9, 3 * HEADS + 1)),
         ],
         compiler_params=pltpu.CompilerParams(
             collective_id=0, has_side_effects=True, vmem_limit_bytes=62 * 1024 * 1024

time: 116 us -> 120 us (1.034)
  Pallas kernels: 113 us -> 117 us
    pallas_call x1, Pallas kernels: 113 us -> 117 us  [body(): pl.pallas_call(kernel, out_shape=(jax.ShapeDtypeStruct((rows, SHARD), BF1...]
where the time goes in v6:
time: 120 us; the launch traced here: 119 us
  Pallas kernels  117 us (98%)
  local copies, waits for them, and re-layouts  2.23 us (2%)
    pallas_call x1, Pallas kernels, body(): pl.pallas_call(kernel, out_shape=(jax.ShapeDtypeStruct((rows, SHARD), BF1...  117 us

profile of v6, /device:TPU:14, one launch (start us, length us, event | category | flops | bytes accessed | tf_op | source)
XLA Modules:
  0.0 119.5 jit_solution(4900966897735286682)
XLA Ops:
  0.0 117.3 %shard_map.100 = (bf16[768,640]{1,0:T(8,128)(2,1)}, bf16[3,8,128,640]{3,2,1,0:T(8,128)(2,1)}) custom-call(bf16[768,640]{1,0:T(8,128)(2,1)} %tok.1, s32[10,96]{1,0:T(8,128)} %bitcast.11, s32[10,96]{1,0:T(8,128)} %bitcast.12, s32[96]{0:T(128)} %mbf.1, f32[8,128]{1,0:T(8,128)} %constant.2.clone.consts, bf16[3,5120,384]{2,1,0:T(8,128)(2,1)} %bitcast.6, ...), custom_call_target="tpu_custom_call" | custom-call | tf_op jit(solution)/shard_map/pallas_call | solution.py:626
  117.3 2.2 %copy.12 = bf16[768,640]{1,0:T(8,128)(2,1)} copy(bf16[768,640]{1,0:T(8,128)(2,1)} %get-tuple-element.6) | data formatting | bytes 1966080
